TPU v7x, 32 devices: a whole 2x2x4 slice. The times are simulated.
32 devices in a mesh: seq: 2 (over core), grp: 16 (over z, y, x).
Axes of the slice: x: 2, y: 2, z: 4, core: 2. Of those that a mesh axis runs over, the one named last changes fastest.
Arguments:
- inputs: bfloat16 [2, 16, 1024, 768], P(None, 'grp', 'seq'), may hold values from -6 to 6
- cotangent: bfloat16 [2, 16, 1024, 768], P(None, 'grp', 'seq'), may hold values from -6 to 6
- query_weight: bfloat16 [768, 768], P(('seq', 'grp')), may hold values from -0.3125 to 0.3125
- query_bias: bfloat16 [768], P(('seq', 'grp')), may hold values from -1.5 to 1.5
- key_weight: bfloat16 [768, 768], P(('seq', 'grp')), may hold values from -0.3125 to 0.3125
- value_weight: bfloat16 [768, 768], P(('seq', 'grp')), may hold values from -0.21875 to 0.21875
- value_bias: bfloat16 [768], P(('seq', 'grp')), may hold values from -1.5 to 1.5
- output_weight: bfloat16 [768, 768], P(('seq', 'grp')), may hold values from -1.25 to 1.25
- output_bias: bfloat16 [768], P(('seq', 'grp')), may hold values from -1.5 to 1.5
- first_gain: bfloat16 [768], P(('seq', 'grp')), may hold values from 0.5 to 1.5
- first_shift: bfloat16 [768], P(('seq', 'grp')), may hold values from -1.5 to 1.5
- inner_weight: bfloat16 [768, 3072], P(('seq', 'grp')), may hold values from -0.21875 to 0.21875
- inner_bias: bfloat16 [3072], P(('seq', 'grp')), may hold values from -1.5 to 1.5
- outer_weight: bfloat16 [3072, 768], P(('seq', 'grp')), may hold values from -0.109375 to 0.109375
- outer_bias: bfloat16 [768], P(('seq', 'grp')), may hold values from -1.5 to 1.5
- second_gain: bfloat16 [768], P(('seq', 'grp')), may hold values from 0.5 to 1.5
- second_shift: bfloat16 [768], P(('seq', 'grp')), may hold values from -1.5 to 1.5
Outputs:
- layer_out: bfloat16 [2, 16, 1024, 768], P(None, 'grp', 'seq')
- input_gradient: bfloat16 [2, 16, 1024, 768], P(None, 'grp', 'seq')
- query_weight_gradient: float32 [768, 768], P(('seq', 'grp'))
- query_bias_gradient: float32 [768], P(('seq', 'grp'))
- key_weight_gradient: float32 [768, 768], P(('seq', 'grp'))
- value_weight_gradient: float32 [768, 768], P(('seq', 'grp'))
- value_bias_gradient: float32 [768], P(('seq', 'grp'))
- output_weight_gradient: float32 [768, 768], P(('seq', 'grp'))
- output_bias_gradient: float32 [768], P(('seq', 'grp'))
- first_gain_gradient: float32 [768], P(('seq', 'grp'))
- first_shift_gradient: float32 [768], P(('seq', 'grp'))
- inner_weight_gradient: float32 [768, 3072], P(('seq', 'grp'))
- inner_bias_gradient: float32 [3072], P(('seq', 'grp'))
- outer_weight_gradient: float32 [3072, 768], P(('seq', 'grp'))
- outer_bias_gradient: float32 [768], P(('seq', 'grp'))
- second_gain_gradient: float32 [768], P(('seq', 'grp'))
- second_shift_gradient: float32 [768], P(('seq', 'grp'))
All inputs are finite; a program needn't handle non-finite values.
Results may differ from a plain program's by a relative error of at most 0.015.
The roundings to bfloat16 on the way count: a program that leaves them out, or rounds other values in their place, can miss the bound.
Values may be sent and summed in bfloat16 or wider, within the bound.
A program may use at most 192 MiB of HBM per device.

v0:
```python
import jax
import jax.numpy as jnp
from jax import lax
from jax.sharding import PartitionSpec as P

HEADS = 12
BLOCK = 512


SCALE_FACTOR = 0.125


def norm_rows(rows, gain, shift):
    average = jnp.mean(rows, axis=-1, keepdims=True)
    centred = rows - average
    variance = jnp.mean(centred * centred, axis=-1, keepdims=True)
    return centred * lax.rsqrt(variance + 1e-05) * gain + shift


def gelu_tanh(values):
    return jax.nn.gelu(values, approximate=True)


def matmul(left, right):
    return jnp.dot(left, right, preferred_element_type=jnp.float32)


def left_inner(left, right):
    return lax.dot_general(
        left, right, (((0,), (0,)), ((), ())), preferred_element_type=jnp.float32
    )


def right_inner(left, right):
    return lax.dot_general(
        left, right, (((1,), (1,)), ((), ())), preferred_element_type=jnp.float32
    )


def split_heads(values):
    return values.reshape(values.shape[0], HEADS, -1)


def block_scores(queries, key_block):
    return (
        jnp.einsum("qhd,khd->hqk", queries, key_block, preferred_element_type=jnp.float32)
        * SCALE_FACTOR
    )


def attention_forward(queries, keys, values):
    rows = queries.shape[0]
    count = keys.shape[0] // BLOCK
    key_blocks = keys.reshape(count, BLOCK, HEADS, -1)
    value_blocks = values.reshape(count, BLOCK, HEADS, -1)

    def running(carry, key_block):
        top, total = carry
        scores = block_scores(queries, key_block)
        new_top = jnp.maximum(top, jnp.max(scores, axis=-1))
        total = total * jnp.exp(top - new_top) + jnp.sum(
            jnp.exp(scores - new_top[..., None]), axis=-1
        )
        return ((new_top, total), None)

    start = (jnp.full((HEADS, rows), -jnp.inf, jnp.float32), jnp.zeros((HEADS, rows), jnp.float32))
    (top, total), unused = lax.scan(running, start, key_blocks)
    log_total = top + jnp.log(total)

    def weighted(summed, pair):
        key_block, value_block = pair
        probs = jnp.exp(block_scores(queries, key_block) - log_total[..., None]).astype(
            jnp.bfloat16
        )
        summed = summed + jnp.einsum(
            "hqk,khd->qhd", probs, value_block, preferred_element_type=jnp.float32
        )
        return (summed, None)

    mixed, unused = lax.scan(
        weighted, jnp.zeros(queries.shape, jnp.float32), (key_blocks, value_blocks)
    )
    return (mixed, log_total)


def attention_backward(queries, keys, values, mixed_grad, log_total):
    rows = queries.shape[0]
    count = keys.shape[0] // BLOCK
    key_blocks = keys.reshape(count, BLOCK, HEADS, -1)
    value_blocks = values.reshape(count, BLOCK, HEADS, -1)

    def block_parts(key_block, value_block):
        probs = jnp.exp(block_scores(queries, key_block) - log_total[..., None])
        slopes = jnp.einsum(
            "qhd,khd->hqk", mixed_grad, value_block, preferred_element_type=jnp.float32
        )
        return (probs, slopes)

    def first_pass(summed, pair):
        probs, slopes = block_parts(pair[0], pair[1])
        return (summed + jnp.sum(probs * slopes, axis=-1), None)

    offset, unused = lax.scan(
        first_pass, jnp.zeros((HEADS, rows), jnp.float32), (key_blocks, value_blocks)
    )

    def second_pass(summed, pair):
        key_block, value_block = pair
        probs, slopes = block_parts(key_block, value_block)
        score_grad = (probs * (slopes - offset[..., None])).astype(jnp.bfloat16)
        summed = summed + jnp.einsum(
            "hqk,khd->qhd", score_grad, key_block, preferred_element_type=jnp.float32
        )
        key_part = jnp.einsum(
            "hqk,qhd->khd", score_grad, queries, preferred_element_type=jnp.float32
        )
        value_part = jnp.einsum(
            "hqk,qhd->khd",
            probs.astype(jnp.bfloat16),
            mixed_grad,
            preferred_element_type=jnp.float32,
        )
        return (summed, (key_part, value_part))

    query_grad, parts = lax.scan(
        second_pass, jnp.zeros(queries.shape, jnp.float32), (key_blocks, value_blocks)
    )
    length = keys.shape[0]
    query_grad = query_grad.reshape(rows, -1) * SCALE_FACTOR
    return (
        query_grad,
        parts[0].reshape(length, -1) * SCALE_FACTOR,
        parts[1].reshape(length, -1),
        offset,
    )


def forward_slice(tokens, params):
    (
        query_weight,
        query_bias,
        key_weight,
        value_weight,
        value_bias,
        output_weight,
        output_bias,
        first_gain,
        first_shift,
        inner_weight,
        inner_bias,
        outer_weight,
        outer_bias,
        second_gain,
        second_shift,
    ) = params
    rows = tokens.shape[0]
    queries = (matmul(tokens, query_weight) + query_bias.astype(jnp.float32)).astype(jnp.bfloat16)
    keys = matmul(tokens, key_weight).astype(jnp.bfloat16)
    values = (matmul(tokens, value_weight) + value_bias.astype(jnp.float32)).astype(jnp.bfloat16)
    all_keys, all_values = (
        lax.all_gather(keys, "seq", axis=0, tiled=True),
        lax.all_gather(values, "seq", axis=0, tiled=True),
    )
    mixed, log_total = attention_forward(
        split_heads(queries), split_heads(all_keys), split_heads(all_values)
    )
    attended = mixed.reshape(rows, -1).astype(jnp.bfloat16)
    first_sum = (
        tokens.astype(jnp.float32)
        + matmul(attended, output_weight)
        + output_bias.astype(jnp.float32)
    )
    hidden = norm_rows(first_sum, first_gain.astype(jnp.float32), first_shift.astype(jnp.float32))
    hidden_low = hidden.astype(jnp.bfloat16)
    inner = matmul(hidden_low, inner_weight) + inner_bias.astype(jnp.float32)
    active = gelu_tanh(inner).astype(jnp.bfloat16)
    second_sum = hidden + matmul(active, outer_weight) + outer_bias.astype(jnp.float32)
    result = norm_rows(
        second_sum, second_gain.astype(jnp.float32), second_shift.astype(jnp.float32)
    )
    kept = (tokens, queries, log_total, attended, first_sum, hidden_low, inner, active, second_sum)
    return (result.astype(jnp.bfloat16), kept, (all_keys, all_values))


def backward_slice(upstream, kept, params, all_keys, all_values):
    (
        query_weight,
        query_bias,
        key_weight,
        value_weight,
        value_bias,
        output_weight,
        output_bias,
        first_gain,
        first_shift,
        inner_weight,
        inner_bias,
        outer_weight,
        outer_bias,
        second_gain,
        second_shift,
    ) = params
    tokens, queries, log_total, attended, first_sum, hidden_low, inner, active, second_sum = kept
    unused, second_pull = jax.vjp(
        norm_rows, second_sum, second_gain.astype(jnp.float32), second_shift.astype(jnp.float32)
    )
    second_grad, second_gain_grad, second_shift_grad = second_pull(upstream)
    feed_grad = second_grad.astype(jnp.bfloat16)
    outer_weight_grad = left_inner(active, feed_grad)
    outer_bias_grad = jnp.sum(feed_grad.astype(jnp.float32), axis=0)
    unused, gelu_pull = jax.vjp(gelu_tanh, inner)
    inner_grad = gelu_pull(right_inner(feed_grad, outer_weight))[0].astype(jnp.bfloat16)
    inner_weight_grad = left_inner(hidden_low, inner_grad)
    inner_bias_grad = jnp.sum(inner_grad.astype(jnp.float32), axis=0)
    hidden_grad = second_grad + right_inner(inner_grad, inner_weight)
    unused, first_pull = jax.vjp(
        norm_rows, first_sum, first_gain.astype(jnp.float32), first_shift.astype(jnp.float32)
    )
    first_grad, first_gain_grad, first_shift_grad = first_pull(hidden_grad)
    branch_grad = first_grad.astype(jnp.bfloat16)
    output_weight_grad = left_inner(attended, branch_grad)
    output_bias_grad = jnp.sum(branch_grad.astype(jnp.float32), axis=0)
    mixed_grad = right_inner(branch_grad, output_weight).astype(jnp.bfloat16)
    query_part, key_terms, value_terms, offset = attention_backward(
        split_heads(queries),
        split_heads(all_keys),
        split_heads(all_values),
        split_heads(mixed_grad),
        log_total,
    )
    key_sum, value_sum = (
        lax.psum_scatter(
            key_terms.astype(jnp.bfloat16), "seq", scatter_dimension=0, tiled=True
        ).astype(jnp.float32),
        lax.psum_scatter(
            value_terms.astype(jnp.bfloat16), "seq", scatter_dimension=0, tiled=True
        ).astype(jnp.float32),
    )
    query_grad = query_part.astype(jnp.bfloat16)
    key_grad = key_sum.astype(jnp.bfloat16)
    value_grad = value_sum.astype(jnp.bfloat16)
    query_weight_grad = left_inner(tokens, query_grad)
    key_weight_grad = left_inner(tokens, key_grad)
    value_weight_grad = left_inner(tokens, value_grad)
    query_bias_grad = jnp.sum(query_grad.astype(jnp.float32), axis=0)
    value_bias_grad = jnp.sum(value_grad.astype(jnp.float32), axis=0)
    input_rows = (
        first_grad
        + right_inner(query_grad, query_weight)
        + right_inner(key_grad, key_weight)
        + right_inner(value_grad, value_weight)
    )
    grads = (
        query_weight_grad,
        query_bias_grad,
        key_weight_grad,
        value_weight_grad,
        value_bias_grad,
        output_weight_grad,
        output_bias_grad,
        first_gain_grad,
        first_shift_grad,
        inner_weight_grad,
        inner_bias_grad,
        outer_weight_grad,
        outer_bias_grad,
        second_gain_grad,
        second_shift_grad,
    )
    return (input_rows.astype(jnp.bfloat16), grads)


def body(
    inputs,
    cotangent,
    query_weight,
    query_bias,
    key_weight,
    value_weight,
    value_bias,
    output_weight,
    output_bias,
    first_gain,
    first_shift,
    inner_weight,
    inner_bias,
    outer_weight,
    outer_bias,
    second_gain,
    second_shift,
):
    shards = (
        query_weight,
        query_bias,
        key_weight,
        value_weight,
        value_bias,
        output_weight,
        output_bias,
        first_gain,
        first_shift,
        inner_weight,
        inner_bias,
        outer_weight,
        outer_bias,
        second_gain,
        second_shift,
    )
    micro = inputs.shape[0]
    devices = lax.axis_size(("seq", "grp"))
    stored = []
    out_rows = []
    for index in range(micro):
        params = (
            lax.all_gather(shards[0], ("seq", "grp"), axis=0, tiled=True),
            lax.all_gather(shards[1], ("seq", "grp"), axis=0, tiled=True),
            lax.all_gather(shards[2], ("seq", "grp"), axis=0, tiled=True),
            lax.all_gather(shards[3], ("seq", "grp"), axis=0, tiled=True),
            lax.all_gather(shards[4], ("seq", "grp"), axis=0, tiled=True),
            lax.all_gather(shards[5], ("seq", "grp"), axis=0, tiled=True),
            lax.all_gather(shards[6], ("seq", "grp"), axis=0, tiled=True),
            lax.all_gather(shards[7], ("seq", "grp"), axis=0, tiled=True),
            lax.all_gather(shards[8], ("seq", "grp"), axis=0, tiled=True),
            lax.all_gather(shards[9], ("seq", "grp"), axis=0, tiled=True),
            lax.all_gather(shards[10], ("seq", "grp"), axis=0, tiled=True),
            lax.all_gather(shards[11], ("seq", "grp"), axis=0, tiled=True),
            lax.all_gather(shards[12], ("seq", "grp"), axis=0, tiled=True),
            lax.all_gather(shards[13], ("seq", "grp"), axis=0, tiled=True),
            lax.all_gather(shards[14], ("seq", "grp"), axis=0, tiled=True),
        )
        result, kept, gathered = forward_slice(inputs[index, 0], params)
        out_rows.append(result)
        stored.append((kept, gathered))
    gradients = tuple(
        (jnp.zeros((piece.shape[0] * devices,) + piece.shape[1:], jnp.float32) for piece in shards)
    )
    grad_rows = []
    for index in range(micro):
        params = (
            lax.all_gather(shards[0], ("seq", "grp"), axis=0, tiled=True),
            lax.all_gather(shards[1], ("seq", "grp"), axis=0, tiled=True),
            lax.all_gather(shards[2], ("seq", "grp"), axis=0, tiled=True),
            lax.all_gather(shards[3], ("seq", "grp"), axis=0, tiled=True),
            lax.all_gather(shards[4], ("seq", "grp"), axis=0, tiled=True),
            lax.all_gather(shards[5], ("seq", "grp"), axis=0, tiled=True),
            lax.all_gather(shards[6], ("seq", "grp"), axis=0, tiled=True),
            lax.all_gather(shards[7], ("seq", "grp"), axis=0, tiled=True),
            lax.all_gather(shards[8], ("seq", "grp"), axis=0, tiled=True),
            lax.all_gather(shards[9], ("seq", "grp"), axis=0, tiled=True),
            lax.all_gather(shards[10], ("seq", "grp"), axis=0, tiled=True),
            lax.all_gather(shards[11], ("seq", "grp"), axis=0, tiled=True),
            lax.all_gather(shards[12], ("seq", "grp"), axis=0, tiled=True),
            lax.all_gather(shards[13], ("seq", "grp"), axis=0, tiled=True),
            lax.all_gather(shards[14], ("seq", "grp"), axis=0, tiled=True),
        )
        kept, gathered = stored[index]
        local_tokens = kept[0]
        keys = matmul(local_tokens, params[2]).astype(jnp.bfloat16)
        values = (matmul(local_tokens, params[3]) + params[4].astype(jnp.float32)).astype(
            jnp.bfloat16
        )
        all_keys, all_values = (
            lax.all_gather(keys, "seq", axis=0, tiled=True),
            lax.all_gather(values, "seq", axis=0, tiled=True),
        )
        upstream = cotangent[index, 0].astype(jnp.float32)
        input_rows, grads = backward_slice(upstream, kept, params, all_keys, all_values)
        grad_rows.append(input_rows)
        gradients = tuple((total + part for total, part in zip(gradients, grads)))
    reduced = lax.psum_scatter(gradients, ("seq", "grp"), scatter_dimension=0, tiled=True)
    layer_out = jnp.stack(out_rows)[:, None]
    input_gradient = jnp.stack(grad_rows)[:, None]
    return (layer_out, input_gradient) + tuple(reduced)


def solution(mesh):
    placed = (
        P(None, "grp", "seq", None),
        P(None, "grp", "seq", None),
        P(("seq", "grp"), None),
        P(("seq", "grp")),
        P(("seq", "grp"), None),
        P(("seq", "grp"), None),
        P(("seq", "grp")),
        P(("seq", "grp"), None),
        P(("seq", "grp")),
        P(("seq", "grp")),
        P(("seq", "grp")),
        P(("seq", "grp"), None),
        P(("seq", "grp")),
        P(("seq", "grp"), None),
        P(("seq", "grp")),
        P(("seq", "grp")),
        P(("seq", "grp")),
    )
    return jax.shard_map(
        body,
        mesh=mesh,
        in_specs=placed,
        out_specs=(
            P(None, "grp", "seq", None),
            P(None, "grp", "seq", None),
            P(("seq", "grp"), None),
            P(("seq", "grp")),
            P(("seq", "grp"), None),
            P(("seq", "grp"), None),
            P(("seq", "grp")),
            P(("seq", "grp"), None),
            P(("seq", "grp")),
            P(("seq", "grp")),
            P(("seq", "grp")),
            P(("seq", "grp"), None),
            P(("seq", "grp")),
            P(("seq", "grp"), None),
            P(("seq", "grp")),
            P(("seq", "grp")),
            P(("seq", "grp")),
        ),
        check_vma=False,
    )
```

profile of v0, /device:TPU:0, one launch (start us, length us, event | category | flops | bytes accessed | tf_op | source)
XLA Modules:
  0.0 1374.1 jit_solution(11453247216769947716)
XLA Ops:
  9.6 58.2 %all-gather.15.cloned.1.call-done = bf16[768,768]{1,0:T(8,128)(2,1)} async-done(((bf16[24,768]{1,0:T(8,128)(2,1)}), bf16[768,768]{1,0:T(8,128)(2,1)}) %all-gather.15.cloned.1.call-update) | async-done | bytes 1179664 | tf_op jit(solution)/shard_map/all_gather | solution.py:317
  73.2 39.7 %all-reduce.19 = (bf16[768]{0:T(1024)(128)(2,1)S(1)}, bf16[768]{0:T(1024)(128)(2,1)S(1)}, bf16[768]{0:T(1024)(128)(2,1)S(1)}, bf16[768]{0:T(1024)(128)(2,1)S(1)}...) all-reduce(bf16[768]{0:T(1024)(128)(2,1)S(1)} %dynamic-update-slice, ...), channel_id=1, replica_groups=mesh['seq'=2,'grp'=16] {'seq','grp'}, use_global_device_ids=true, to_apply=%add | all-reduce | flops 9216 | bytes 36864
  112.8 10.8 all-gather.11.cloned.1.call-done
  139.0 40.6 %all-gather.19.cloned.1.call-done = bf16[768,768]{1,0:T(8,128)(2,1)} async-done(((bf16[24,768]{1,0:T(8,128)(2,1)}), bf16[768,768]{1,0:T(8,128)(2,1)}) %all-gather.19.cloned.1.call-update) | async-done | bytes 1179664 | tf_op jit(solution)/shard_map/all_gather | solution.py:315
  199.6 29.6 %while.102 = (s32[]{:T(128)}, f32[12,512]{1,0:T(8,128)S(1)}, f32[12,512]{1,0:T(8,128)S(1)}, bf16[2,512,12,64]{1,3,2,0:T(8,128)(2,1)}, bf16[512,12,64]{0,2,1:T(8,128)(2,1)S(1)}, /*index=5*/s32[]{:T(128)}, s32[]{:T(128)}) while((s32[]{:T(128)}, f32[12,512]{1,0:T(8,128)S(1)}, f32[12,512]{1,0:T(8,128)S(1)}, ...), condition=%wide.region_13.14_spmd.clone, body=%wide.region_10.13_spmd.clone.sunk | while | flops 418412544 | bytes 27058776 | solution.py:67
  238.6 12.2 while.103
  272.2 28.8 %while.100 = (s32[]{:T(128)}, f32[12,512]{1,0:T(8,128)S(1)}, f32[12,512]{1,0:T(8,128)S(1)}, bf16[2,512,12,64]{1,3,2,0:T(8,128)(2,1)}, bf16[512,12,64]{0,2,1:T(8,128)(2,1)S(1)}, /*index=5*/s32[]{:T(128)}, s32[]{:T(128)}) while((s32[]{:T(128)}, f32[12,512]{1,0:T(8,128)S(1)}, f32[12,512]{1,0:T(8,128)S(1)}, ...), condition=%wide.region_3.4_spmd.clone, body=%wide.region_0.3_spmd.clone.sunk | while | flops 418412544 | bytes 27058776 | solution.py:67
  301.0 12.4 while.101
  322.2 28.5 %all-gather.23.cloned.1.call-done = bf16[768,3072]{1,0:T(8,128)(2,1)} async-done(((bf16[24,3072]{1,0:T(8,128)(2,1)}), bf16[768,3072]{1,0:T(8,128)(2,1)}) %all-gather.23.cloned.1.call-update) | async-done | bytes 4718608 | tf_op jit(solution)/shard_map/all_gather | solution.py:324
  350.7 8.1 fusion.156
  358.8 57.0 %all-gather.25.cloned.1.call-done = bf16[3072,768]{1,0:T(8,128)(2,1)} async-done(((bf16[96,768]{1,0:T(8,128)(2,1)}), bf16[3072,768]{1,0:T(8,128)(2,1)}) %all-gather.25.cloned.1.call-update) | async-done | bytes 4718608 | tf_op jit(solution)/shard_map/all_gather | solution.py:326
  415.8 8.9 fusion.173
  445.7 17.9 %convert_reduce_fusion.1 = (f32[3072]{0:T(1024)}, bf16[512,3072]{1,0:T(8,128)(2,1)}, f32[3072]{0:T(1024)}, bf16[512,3072]{1,0:T(8,128)(2,1)S(1)}) fusion(f32[512,3072]{1,0:T(8,128)} %copy-done.104, f32[3072]{0:T(1024)S(1)} %convert_element_type.252, f32[512,3072]{1,0:T(8,128)} %fusion.176, f32[512,3072]{1,0:T(8,128)} %fusion.156, ...), kind=kOutput, calls=%fused_computation.123 | convolution fusion | flops 2488264704 | bytes 30707712 | tf_op jit(solution)/shard_map/dot_general | solution.py:35
  476.9 13.0 while.104
  492.0 54.9 %while.105 = (s32[]{:T(128)}, f32[512,12,64]{0,2,1:T(8,128)}, f32[2,512,12,64]{1,3,2,0:T(8,128)}, bf16[2,512,12,64]{1,3,2,0:T(8,128)(2,1)}, bf16[2,512,12,64]{1,...) while((s32[]{:T(128)}, f32[512,12,64]{0,2,1:T(8,128)}, ...), condition=%wide.region_28.29_spmd.clone, body=%wide.region_27.28_spmd.clone.sunk | while | flops 2039218176 | bytes 143993520 | solution.py:125
  556.8 13.4 while.106
  572.2 54.8 %while.107 = (s32[]{:T(128)}, f32[512,12,64]{0,2,1:T(8,128)}, f32[2,512,12,64]{1,3,2,0:T(8,128)}, bf16[2,512,12,64]{1,3,2,0:T(8,128)(2,1)}, bf16[2,512,12,64]{1,...) while((s32[]{:T(128)}, f32[512,12,64]{0,2,1:T(8,128)}, ...), condition=%wide.region_39.40_spmd.clone, body=%wide.region_38.39_spmd.clone.sunk | while | flops 2039218176 | bytes 143993520 | solution.py:125
  684.1 10.4 convolution_add_fusion
  714.7 40.4 %all-reduce.18 = (f32[768]{0:T(1024)S(1)}, f32[768]{0:T(1024)S(1)}, f32[768]{0:T(1024)S(1)}, f32[768]{0:T(1024)S(1)}, f32[768]{0:T(1024)S(1)}, /*index=5*/f32[30...) all-reduce(f32[768]{0:T(1024)S(1)} %add.399, ...), channel_id=7, replica_groups=mesh['seq'=2,'grp'=16] {'seq','grp'}, use_global_device_ids=true, to_apply=%region_45.46.clone | all-reduce | flops 9216 | bytes 73728
  770.8 104.7 %reduce-scatter.31.cloned.1.call-done = f32[24,768]{1,0:T(8,128)} async-done(((f32[768,768]{1,0:T(8,128)}), f32[24,768]{1,0:T(8,128)}) %reduce-scatter.31.cloned.1.call-update) | async-done | bytes 73744
  875.5 103.8 %reduce-scatter.35.cloned.1.call-done = f32[24,768]{1,0:T(8,128)} async-done(((f32[768,768]{1,0:T(8,128)}), f32[24,768]{1,0:T(8,128)}) %reduce-scatter.35.cloned.1.call-update) | async-done | bytes 73744
  979.3 104.7 %reduce-scatter.33.cloned.1.call-done = f32[24,768]{1,0:T(8,128)} async-done(((f32[768,768]{1,0:T(8,128)}), f32[24,768]{1,0:T(8,128)}) %reduce-scatter.33.cloned.1.call-update) | async-done | bytes 73744
  1084.0 141.0 %reduce-scatter.29.cloned.1.call-done = f32[96,768]{1,0:T(8,128)} async-done(((f32[3072,768]{1,0:T(8,128)}), f32[96,768]{1,0:T(8,128)}) %reduce-scatter.29.cloned.1.call-update) | async-done | bytes 294928 | tf_op jit(solution)/shard_map/reduce_scatter | solution.py:370
  1225.0 141.9 %reduce-scatter.27.cloned.1.call-done = f32[24,3072]{1,0:T(8,128)} async-done(((f32[768,3072]{1,0:T(8,128)}), f32[24,3072]{1,0:T(8,128)}) %reduce-scatter.27.cloned.1.call-update) | async-done | bytes 294928 | tf_op jit(solution)/shard_map/reduce_scatter | solution.py:370
  (493 shorter events, 439.8 us)
Async XLA Ops:
  7.2 60.5 %all-gather.15.cloned.1.call-start = ((), (), s32[]{:S(2)}) async-start(), calls=%async_computation.12 | async-start | bytes 1216512 | tf_op jit(solution)/shard_map/all_gather | solution.py:317
  7.9 115.7 %all-gather.11.cloned.1.call-start = ((), (), s32[]{:S(2)}) async-start(), calls=%async_computation.10 | async-start | bytes 1216512 | tf_op jit(solution)/shard_map/all_gather | solution.py:318
  8.7 170.9 %all-gather.19.cloned.1.call-start = ((), (), s32[]{:S(2)}) async-start(), calls=%async_computation.14 | async-start | bytes 1216512 | tf_op jit(solution)/shard_map/all_gather | solution.py:315
  9.5 180.3 %all-gather.29.cloned.1.call-start = ((), (), s32[]{:S(2)}) async-start(), calls=%async_computation.19 | async-start | bytes 2359296 | tf_op jit(solution)/shard_map/all_gather | solution.py:161
  70.9 158.3 %all-gather.27.cloned.1.call-start = ((), (), s32[]{:S(2)}) async-start(), calls=%async_computation.18 | async-start | bytes 2359296 | tf_op jit(solution)/shard_map/all_gather | solution.py:162
  126.6 127.0 %all-gather.17.cloned.1.call-start = ((), (), s32[]{:S(2)}) async-start(), calls=%async_computation.13 | async-start | bytes 2359296 | tf_op jit(solution)/shard_map/all_gather | solution.py:161
  129.7 133.1 %all-gather.13.cloned.1.call-start = ((), (), s32[]{:S(2)}) async-start(), calls=%async_computation.11 | async-start | bytes 2359296 | tf_op jit(solution)/shard_map/all_gather | solution.py:162
  131.5 183.6 %all-gather.21.cloned.1.call-start = ((), (), s32[]{:S(2)}) async-start(), calls=%async_computation.15 | async-start | bytes 1216512 | tf_op jit(solution)/shard_map/all_gather | solution.py:320
  132.2 218.5 %all-gather.23.cloned.1.call-start = ((), (), s32[]{:S(2)}) async-start(), calls=%async_computation.16 | async-start | bytes 4866048 | tf_op jit(solution)/shard_map/all_gather | solution.py:324
  133.0 282.9 %all-gather.25.cloned.1.call-start = ((), (), s32[]{:S(2)}) async-start(), calls=%async_computation.17 | async-start | bytes 4866048 | tf_op jit(solution)/shard_map/all_gather | solution.py:326
  133.6 521.9 %reduce-scatter.19.cloned.1.call-start = ((), (), s32[]{:S(2)}) async-start(), calls=%async_computation.21 | async-start | bytes 2359296 | tf_op jit(solution)/shard_map/reduce_scatter | solution.py:235
  137.7 333.4 %copy-start.57 = (f32[768]{0:T(1024)}, f32[768]{0:T(1024)S(1)}, u32[]{:S(2)}) copy-start(f32[768]{0:T(1024)S(1)} %convert_element_type.249) | copy-start | bytes 9220
  137.8 291.1 %copy-start.59 = (f32[768]{0:T(1024)}, f32[768]{0:T(1024)S(1)}, u32[]{:S(2)}) copy-start(f32[768]{0:T(1024)S(1)} %convert_element_type.250) | copy-start | bytes 9220
  137.8 307.9 %copy-start.79 = (f32[3072]{0:T(1024)}, f32[3072]{0:T(1024)S(1)}, u32[]{:S(2)}) copy-start(f32[3072]{0:T(1024)S(1)} %convert_element_type.252) | copy-start | bytes 36868
  317.8 153.3 %copy-start.61 = (f32[512]{0:T(512)}, f32[512]{0:T(512)S(1)}, u32[]{:S(2)}) copy-start(f32[512]{0:T(512)S(1)} %broadcast_multiply_fusion.1) | copy-start | bytes 6148
  551.6 107.2 %reduce-scatter.23.cloned.1.call-start = ((), (), s32[]{:S(2)}) async-start(), calls=%async_computation.23 | async-start | bytes 2359296 | tf_op jit(solution)/shard_map/reduce_scatter | solution.py:235
  631.7 34.7 %reduce-scatter.17.cloned.1.call-start = ((), (), s32[]{:S(2)}) async-start(), calls=%async_computation.20 | async-start | bytes 2359296 | tf_op jit(solution)/shard_map/reduce_scatter | solution.py:232
  636.2 33.6 %reduce-scatter.21.cloned.1.call-start = ((), (), s32[]{:S(2)}) async-start(), calls=%async_computation.22 | async-start | bytes 2359296 | tf_op jit(solution)/shard_map/reduce_scatter | solution.py:232
  641.1 129.7 %reduce-scatter.25.cloned.1.call-start = ((), (), s32[]{:S(2)}) async-start(), calls=%async_computation.24 | async-start | bytes 2433024 | tf_op jit(solution)/shard_map/reduce_scatter | solution.py:370
  645.5 230.0 %reduce-scatter.31.cloned.1.call-start = ((), (), s32[]{:S(2)}) async-start(), calls=%async_computation.27 | async-start | bytes 2433024
  655.4 323.9 %reduce-scatter.35.cloned.1.call-start = ((), (), s32[]{:S(2)}) async-start(), calls=%async_computation.29 | async-start | bytes 2433024
  666.3 417.7 %reduce-scatter.33.cloned.1.call-start = ((), (), s32[]{:S(2)}) async-start(), calls=%async_computation.28 | async-start | bytes 2433024
  677.0 548.0 %reduce-scatter.29.cloned.1.call-start = ((), (), s32[]{:S(2)}) async-start(), calls=%async_computation.26 | async-start | bytes 9732096 | tf_op jit(solution)/shard_map/reduce_scatter | solution.py:370
  694.6 672.3 %reduce-scatter.27.cloned.1.call-start = ((), (), s32[]{:S(2)}) async-start(), calls=%async_computation.25 | async-start | bytes 9732096 | tf_op jit(solution)/shard_map/reduce_scatter | solution.py:370
  (110 other events, 1450.1 us)
Sparse Core Ops, SparseCore 0:
  10.9 56.7 all-gather.14
  70.6 52.9 all-gather.10
  126.5 53.0 all-gather.18
  181.0 8.7 all-gather.28
  191.2 10.9 all-gather.26
  203.6 10.9 all-gather.16
  216.1 10.9 all-gather.12
  230.0 55.2 all-gather.20
  288.2 62.4 all-gather.22
  353.4 62.3 all-gather.24
  551.7 7.8 reduce-scatter.18
  631.8 7.9 reduce-scatter.22
  642.0 10.2 reduce-scatter.16
  654.5 10.2 reduce-scatter.20
  670.5 100.2 reduce-scatter.24
  777.4 98.0 reduce-scatter.30
  881.2 98.0 reduce-scatter.34
  985.8 98.1 reduce-scatter.32
  1090.5 134.4 reduce-scatter.28
  1232.3 134.4 reduce-scatter.26
where the time goes:
time: 1380 us; the launch traced here: 1370 us
  waiting for transfers between devices  803 us (58%)
  matrix products  309 us (22%)
  local copies, waits for them, and re-layouts  113 us (8%)
  blocking collectives  80.1 us (6%)
  other arithmetic  50.5 us (4%)
  between operations  16.3 us (1%)
    unnamed x23, waiting for transfers between devices  317 us
    reduce_scatter x3, waiting for transfers between devices, body(): lax.psum_scatter(gradients, ('seq', 'grp'), scatter_dimension=0, tiled=True)  285 us
    unnamed x2, blocking collectives  80.1 us
    unnamed x243, local copies, waits for them, and re-layouts  61 us
    all_gather x1, waiting for transfers between devices, body(): lax.all_gather(shards[2], ('seq', 'grp'), axis=0, tiled=True)  58.2 us
    all_gather x1, waiting for transfers between devices, body(): lax.all_gather(shards[11], ('seq', 'grp'), axis=0, tiled=True)  57 us
    dot_general x12, matrix products, block_scores(): jnp.einsum('qhd,khd->hqk', queries, key_block, preferred_element_type=jnp...  54.3 us
    dot_general x12, matrix products, left_inner(): lax.dot_general(left, right, (((0,), (0,)), ((), ())), preferred_element_...  48.5 us
  transfers between devices with their start and end apart: 20, of which 12 were waited for; matrix products, arithmetic and copies ran while one was open for 23% of the time, Pallas kernels for 0%

commit v1 on v0

v1 whole, which is shorter than its diff:
```python
import functools

import jax
import jax.numpy as jnp
from jax import lax
from jax.experimental import pallas as pl
from jax.experimental.pallas import tpu as pltpu
from jax.sharding import PartitionSpec as P

HEADS = 12
SCALE = 0.125
EPS = 1e-05
PAIR = 128
ROWS = 256
CHUNK = 768
LANES = 128
VMEM_LIMIT = 64 * 1024 * 1024 - 65536
GELU_C = 0.7978845608028654
GELU_A = 0.044715
MESH = pl.DeviceIdType.MESH
F32 = jnp.float32
BF16 = jnp.bfloat16


def dot_nn(left, right):
    return lax.dot_general(left, right, (((1,), (0,)), ((), ())), preferred_element_type=F32)


def dot_nt(left, right):
    return lax.dot_general(left, right, (((1,), (1,)), ((), ())), preferred_element_type=F32)


def dot_tn(left, right):
    return lax.dot_general(left, right, (((0,), (0,)), ((), ())), preferred_element_type=F32)


def place():
    s = lax.axis_index("seq")
    g = lax.axis_index("grp")
    return s, g // 4, (g // 2) % 2, g % 2


def device(s, z, y, x):
    return (s, z * 4 + y * 2 + x)


def first_partner(s, z, y, x):
    return device(s, z, y * s + (1 - y) * (1 - s), x * (1 - s) + (1 - x) * s)


def second_partner(s, z, y, x):
    return device(s, z, y * (1 - s) + (1 - y) * s, x * s + (1 - x) * (1 - s))


def greet(s, z, y, x):
    barrier = pltpu.get_barrier_semaphore()
    partners = [device(1 - s, z, y, x), first_partner(s, z, y, x), second_partner(s, z, y, x)]
    partners += [device(s, (z + k) % 4, y, x) for k in (1, 2, 3)]
    for partner in partners:
        pl.semaphore_signal(barrier, inc=1, device_id=partner, device_id_type=MESH)
    pl.semaphore_wait(barrier, len(partners))


def remote(src, dst, send, recv, target):
    return pltpu.make_async_remote_copy(
        src_ref=src, dst_ref=dst, send_sem=send, recv_sem=recv, device_id=target, device_id_type=MESH
    )


def gather_kernel(count, *refs):
    shards = refs[:count]
    rows = refs[count]
    fulls = refs[count + 1 : 2 * count + 1]
    all_rows = refs[2 * count + 1]
    own_sem, send, recv, row_own, row_send, row_recv = refs[2 * count + 2 :]
    s, z, y, x = place()
    greet(s, z, y, x)

    def own(a):
        return pltpu.make_async_copy(shards[a], fulls[a].at[s, z, y, x], own_sem.at[a])

    def along_z(a, k):
        return remote(
            shards[a],
            fulls[a].at[s, z, y, x],
            send.at[a, k - 1],
            recv.at[a, k - 1],
            device(s, (z + k) % 4, y, x),
        )

    def first(a):
        part = fulls[a].at[s, :, y, x]
        return remote(part, part, send.at[a, 3], recv.at[a, 3], second_partner(s, z, y, x))

    def second(a, j):
        yy = y * (1 - s) + j * s
        xx = j * (1 - s) + x * s
        part = fulls[a].at[s, :, yy, xx]
        return remote(part, part, send.at[a, 4 + j], recv.at[a, 4 + j], first_partner(s, z, y, x))

    def across(a):
        part = fulls[a].at[s]
        return remote(part, part, send.at[a, 6], recv.at[a, 6], device(1 - s, z, y, x))

    row_copy = remote(rows, all_rows.at[s], row_send, row_recv, device(1 - s, z, y, x))
    row_local = pltpu.make_async_copy(rows, all_rows.at[s], row_own)

    def stage(t, a):
        if t == 0:
            for k in (1, 2, 3):
                along_z(a, k).start()
            own(a).start()
        elif t == 1:
            own(a).wait()
            for k in (1, 2, 3):
                along_z(a, k).wait_recv()
            first(a).start()
        elif t == 2:
            first(a).wait_recv()
            for j in (0, 1):
                second(a, j).start()
        elif t == 3:
            for j in (0, 1):
                second(a, j).wait_recv()
            across(a).start()

    for a in range(count):
        stage(0, a)
    row_copy.start()
    row_local.start()
    for i in range(1, count + 3):
        for t in (3, 2, 1):
            a = i - t
            if 0 <= a < count:
                stage(t, a)
    for a in range(count):
        across(a).wait_recv()
    row_local.wait()
    row_copy.wait()
    for a in range(count):
        for k in (1, 2, 3):
            along_z(a, k).wait_send()
        first(a).wait_send()
        for j in (0, 1):
            second(a, j).wait_send()
        across(a).wait_send()


def gather_box(shards, rows):
    count = len(shards)
    any_spec = pl.BlockSpec(memory_space=pl.ANY)
    vmem_spec = pl.BlockSpec(memory_space=pltpu.VMEM)
    outs = pl.pallas_call(
        functools.partial(gather_kernel, count),
        out_shape=[jax.ShapeDtypeStruct((2, 4, 2, 2) + a.shape, a.dtype) for a in shards]
        + [jax.ShapeDtypeStruct((2,) + rows.shape, rows.dtype)],
        in_specs=[vmem_spec] * (count + 1),
        out_specs=[any_spec] * (count + 1),
        scratch_shapes=[
            pltpu.SemaphoreType.DMA((count,)),
            pltpu.SemaphoreType.DMA((count, 7)),
            pltpu.SemaphoreType.DMA((count, 7)),
            pltpu.SemaphoreType.DMA,
            pltpu.SemaphoreType.DMA,
            pltpu.SemaphoreType.DMA,
        ],
        compiler_params=pltpu.CompilerParams(
            collective_id=1, has_side_effects=True, vmem_limit_bytes=VMEM_LIMIT
        ),
        name="gather_weights",
    )(*shards, rows)
    fulls = [full.reshape((-1, full.shape[-1])) for full in outs[:-1]]
    return fulls, outs[-1]


def scatter_kernel(count, *refs):
    terms = refs[:count]
    outs = refs[count : 2 * count]
    scratch = refs[2 * count :]
    held = scratch[:count]
    got1 = scratch[count : 2 * count]
    got2 = scratch[2 * count : 3 * count]
    got3 = scratch[3 * count : 4 * count]
    got4 = scratch[4 * count : 5 * count]
    load, send, recv = scratch[5 * count :]
    s, z, y, x = place()
    greet(s, z, y, x)
    y2 = y * (1 - s) + (1 - y) * s
    x2 = (1 - x) * (1 - s) + x * s

    def fetch(a):
        return pltpu.make_async_copy(terms[a].at[s], held[a], load.at[a])

    def across(a):
        return remote(
            terms[a].at[1 - s], got1[a], send.at[a, 0], recv.at[a, 0], device(1 - s, z, y, x)
        )

    def first(a, j):
        yy = (1 - y) * (1 - s) + j * s
        xx = j * (1 - s) + (1 - x) * s
        return remote(
            held[a].at[:, yy, xx],
            got2[a].at[:, j],
            send.at[a, 1 + j],
            recv.at[a, 1 + j],
            first_partner(s, z, y, x),
        )

    def second(a):
        return remote(
            held[a].at[:, y2, x2],
            got3[a],
            send.at[a, 3],
            recv.at[a, 3],
            second_partner(s, z, y, x),
        )

    def along_z(a, k):
        zt = (z + k) % 4
        return remote(
            held[a].at[zt, y, x],
            got4[a].at[k - 1],
            send.at[a, 3 + k],
            recv.at[a, 3 + k],
            device(s, zt, y, x),
        )

    def stage(t, a):
        if t == 0:
            across(a).start()
            fetch(a).start()
        elif t == 1:
            fetch(a).wait()
            across(a).wait_recv()

            def add1(i, unused):
                zz, yy, xx = i // 4, (i // 2) % 2, i % 2
                held[a][zz, yy, xx] = (
                    held[a][zz, yy, xx].astype(F32) + got1[a][zz, yy, xx].astype(F32)
                ).astype(BF16)
                return unused

            lax.fori_loop(0, 16, add1, 0)
            for j in (0, 1):
                first(a, j).start()
        elif t == 2:
            for j in (0, 1):
                first(a, j).wait_recv()

            def add2(i, unused):
                zz, j = i // 2, i % 2
                yy = y * (1 - s) + j * s
                xx = j * (1 - s) + x * s
                held[a][zz, yy, xx] = (
                    held[a][zz, yy, xx].astype(F32) + got2[a][zz, j].astype(F32)
                ).astype(BF16)
                return unused

            lax.fori_loop(0, 8, add2, 0)
            second(a).start()
        elif t == 3:
            second(a).wait_recv()

            def add3(zz, unused):
                held[a][zz, y, x] = (
                    held[a][zz, y, x].astype(F32) + got3[a][zz].astype(F32)
                ).astype(BF16)
                return unused

            lax.fori_loop(0, 4, add3, 0)
            for k in (1, 2, 3):
                along_z(a, k).start()
        elif t == 4:
            for k in (1, 2, 3):
                along_z(a, k).wait_recv()
            outs[a][...] = (
                held[a][z, y, x].astype(F32)
                + got4[a][0].astype(F32)
                + got4[a][1].astype(F32)
                + got4[a][2].astype(F32)
            )

    for i in range(count + 4):
        for t in (4, 3, 2, 1, 0):
            a = i - t
            if 0 <= a < count:
                stage(t, a)
    for a in range(count):
        across(a).wait_send()
        for j in (0, 1):
            first(a, j).wait_send()
        second(a).wait_send()
        for k in (1, 2, 3):
            along_z(a, k).wait_send()


def scatter_box(terms):
    count = len(terms)
    any_spec = pl.BlockSpec(memory_space=pl.ANY)
    vmem_spec = pl.BlockSpec(memory_space=pltpu.VMEM)
    sizes = [(term.shape[0] // 32, term.shape[1]) for term in terms]
    shaped = [term.reshape((2, 4, 2, 2) + size) for term, size in zip(terms, sizes)]
    scratch = []
    for lead in ((4, 2, 2), (4, 2, 2), (4, 2), (4,), (3,)):
        scratch += [pltpu.VMEM(lead + size, BF16) for size in sizes]
    scratch += [
        pltpu.SemaphoreType.DMA((count,)),
        pltpu.SemaphoreType.DMA((count, 7)),
        pltpu.SemaphoreType.DMA((count, 7)),
    ]
    return pl.pallas_call(
        functools.partial(scatter_kernel, count),
        out_shape=[jax.ShapeDtypeStruct(size, F32) for size in sizes],
        in_specs=[any_spec] * count,
        out_specs=[vmem_spec] * count,
        scratch_shapes=scratch,
        compiler_params=pltpu.CompilerParams(
            collective_id=2, has_side_effects=True, vmem_limit_bytes=VMEM_LIMIT
        ),
        name="scatter_gradients",
    )(*shaped)


def project_kernel(own_ref, all_ref, wq_ref, wk_ref, wv_ref, vec_ref, q_ref, kv_ref, bias):
    width = wq_ref.shape[1]
    micro = 2

    @pl.when(pl.program_id(0) == 0)
    def _():
        bias[...] = jnp.transpose(vec_ref[...].astype(F32))[:8]

    @pl.when(pl.program_id(0) < micro)
    def _():
        queries = dot_nn(own_ref[0], wq_ref[...]) + bias[0:1]
        q_ref[0] = (queries.astype(BF16).astype(F32) * SCALE).astype(BF16)

    rows = all_ref[0, 0]
    kv_ref[0, 0, :, :width] = dot_nn(rows, wk_ref[...]).astype(BF16)
    kv_ref[0, 0, :, width:] = (dot_nn(rows, wv_ref[...]) + bias[1:2]).astype(BF16)


def project(own, all_rows, wq, wk, wv, vec):
    micro, length, width = own.shape
    parts = all_rows.shape[0]
    whole = lambda a: pl.BlockSpec(a.shape, lambda i: (0,) * a.ndim)
    last = micro - 1
    return pl.pallas_call(
        project_kernel,
        grid=(parts * micro,),
        in_specs=[
            pl.BlockSpec((1, length, width), lambda i: (jnp.minimum(i, last), 0, 0)),
            pl.BlockSpec((1, 1, length, width), lambda i: (i // micro, i % micro, 0, 0)),
            whole(wq),
            whole(wk),
            whole(wv),
            whole(vec),
        ],
        out_specs=[
            pl.BlockSpec((1, length, width), lambda i: (jnp.minimum(i, last), 0, 0)),
            pl.BlockSpec((1, 1, length, 2 * width), lambda i: (i // micro, i % micro, 0, 0)),
        ],
        out_shape=[
            jax.ShapeDtypeStruct((micro, length, width), BF16),
            jax.ShapeDtypeStruct((parts, micro, length, 2 * width), BF16),
        ],
        scratch_shapes=[pltpu.VMEM((8, width), F32)],
        compiler_params=pltpu.CompilerParams(vmem_limit_bytes=VMEM_LIMIT),
        name="project",
    )(own, all_rows, wq, wk, wv, vec)


def head_of(shape):
    return lax.broadcasted_iota(jnp.int32, shape, len(shape) - 1) // 64


def pick(values, head):
    return jnp.where(head_of(values.shape) == head, values, jnp.zeros_like(values))


def attend_kernel(q_ref, k_ref, v_ref, o_ref, lse_ref):
    queries = q_ref[0]
    length = queries.shape[0]
    keys = k_ref[:, 0].reshape(-1, PAIR)
    values = v_ref[:, 0].reshape(-1, PAIR)
    mixed = []
    for head in (0, 1):
        scores = dot_nt(pick(queries, head), keys)
        top = jnp.max(scores, axis=1, keepdims=True)
        powers = jnp.exp(scores - top)
        total = jnp.sum(powers, axis=1, keepdims=True)
        mixed.append(dot_nn(powers.astype(BF16), values) * (1.0 / total))
        column = jnp.broadcast_to(top + jnp.log(total), (length, LANES))
        lse_ref[0, 0, head : head + 1, :] = jnp.transpose(column)[0:1]
    o_ref[0] = jnp.where(head_of(mixed[0].shape) == 0, mixed[0], mixed[1]).astype(BF16)


def attend(queries, kv):
    micro, length, width = queries.shape
    parts = kv.shape[0]
    pairs = width // PAIR
    return pl.pallas_call(
        attend_kernel,
        grid=(micro, pairs),
        in_specs=[
            pl.BlockSpec((1, length, PAIR), lambda m, p: (m, 0, p)),
            pl.BlockSpec((parts, 1, length, PAIR), lambda m, p: (0, m, 0, p)),
            pl.BlockSpec((parts, 1, length, PAIR), lambda m, p: (0, m, 0, pairs + p)),
        ],
        out_specs=[
            pl.BlockSpec((1, length, PAIR), lambda m, p: (m, 0, p)),
            pl.BlockSpec((1, 1, 2, length), lambda m, p: (m, p, 0, 0)),
        ],
        out_shape=[
            jax.ShapeDtypeStruct(queries.shape, BF16),
            jax.ShapeDtypeStruct((micro, pairs, 2, length), F32),
        ],
        compiler_params=pltpu.CompilerParams(vmem_limit_bytes=VMEM_LIMIT),
        name="attend",
    )(queries, kv, kv)


def attend_back_kernel(q_ref, k_ref, v_ref, o_ref, g_ref, lse_ref, dq_ref, dk_ref, dv_ref):
    parts = k_ref.shape[0]
    queries = q_ref[0]
    length = queries.shape[0]
    keys = k_ref[:, 0].reshape(-1, PAIR)
    values = v_ref[:, 0].reshape(-1, PAIR)
    grad = g_ref[0]
    keys_t = jnp.transpose(keys)
    products = jnp.transpose(grad.astype(F32) * o_ref[0].astype(F32))
    dk = jnp.zeros(keys.shape, F32)
    dv = jnp.zeros(keys.shape, F32)
    dq_t = []
    for head in (0, 1):
        offset = jnp.sum(products[64 * head : 64 * head + 64], axis=0, keepdims=True)
        q_head = pick(queries, head)
        g_head = pick(grad, head)
        scores_t = dot_nt(keys, q_head)
        probs_t = jnp.exp(scores_t - lse_ref[0, 0, head : head + 1, :])
        slopes_t = dot_nt(values, g_head)
        score_grad_t = (probs_t * (slopes_t - offset)).astype(BF16)
        dv += dot_nn(probs_t.astype(BF16), g_head)
        dk += dot_nn(score_grad_t, q_head)
        dq_t.append(dot_nn(keys_t[64 * head : 64 * head + 64], score_grad_t))
    dq = jnp.transpose(jnp.concatenate(dq_t, axis=0)) * SCALE
    dq_ref[0] = dq.astype(BF16)
    dk_ref[:, 0] = dk.astype(BF16).reshape(parts, length, PAIR)
    dv_ref[:, 0] = dv.astype(BF16).reshape(parts, length, PAIR)


def attend_back(queries, kv, attended, grad, lse):
    micro, length, width = queries.shape
    parts = kv.shape[0]
    pairs = width // PAIR
    row = pl.BlockSpec((1, length, PAIR), lambda m, p: (m, 0, p))
    col = pl.BlockSpec((parts, 1, length, PAIR), lambda m, p: (0, m, 0, p))
    col2 = pl.BlockSpec((parts, 1, length, PAIR), lambda m, p: (0, m, 0, pairs + p))
    return pl.pallas_call(
        attend_back_kernel,
        grid=(micro, pairs),
        in_specs=[
            row,
            col,
            col2,
            row,
            row,
            pl.BlockSpec((1, 1, 2, length), lambda m, p: (m, p, 0, 0)),
        ],
        out_specs=[row, col, col],
        out_shape=[
            jax.ShapeDtypeStruct((micro, length, width), BF16),
            jax.ShapeDtypeStruct((parts, micro, length, width), BF16),
            jax.ShapeDtypeStruct((parts, micro, length, width), BF16),
        ],
        compiler_params=pltpu.CompilerParams(vmem_limit_bytes=VMEM_LIMIT),
        name="attend_back",
    )(queries, kv, kv, attended, grad, lse)


def mean_rows(values):
    return jnp.mean(values, axis=-1, keepdims=True)


def rows_kernel(
    x_ref,
    att_ref,
    cot_ref,
    wo_ref,
    win_ref,
    wout_ref,
    vec_ref,
    ib_ref,
    out_ref,
    hidden_ref,
    active_ref,
    inner_grad_ref,
    feed_ref,
    branch_ref,
    mixed_ref,
    first_ref,
    vecg_ref,
    ibg_ref,
    vec,
    ib,
    slope,
    vecg,
    ibg,
):
    step = pl.program_id(0)
    chunks = win_ref.shape[1] // CHUNK

    @pl.when(step == 0)
    def _():
        vec[...] = jnp.transpose(vec_ref[...].astype(F32))[:8]
        ib[...] = jnp.transpose(ib_ref[...].astype(F32))[:8]
        vecg[...] = jnp.zeros_like(vecg)
        ibg[...] = jnp.zeros_like(ibg)

    o_b, g1, s1, outer_b, g2, s2 = (vec[i : i + 1] for i in range(2, 8))
    first_sum = x_ref[...].astype(F32) + (dot_nn(att_ref[...], wo_ref[...]) + o_b)
    centred = first_sum - mean_rows(first_sum)
    r1 = lax.rsqrt(mean_rows(centred * centred) + EPS)
    n1 = centred * r1
    hidden = n1 * g1 + s1
    hidden_low = hidden.astype(BF16)
    hidden_ref[...] = hidden_low
    total = hidden + outer_b
    for c in range(chunks):
        cols = slice(c * CHUNK, (c + 1) * CHUNK)
        v = dot_nn(hidden_low, win_ref[:, cols]) + ib[0:1, cols]
        square = v * v
        t = jnp.tanh(v * (GELU_C + (GELU_C * GELU_A) * square))
        half = 0.5 * (1.0 + t)
        active = (v * half).astype(BF16)
        active_ref[:, cols] = active
        slope[:, cols] = half + (0.5 * v) * (1.0 - t * t) * (
            GELU_C + (3.0 * GELU_C * GELU_A) * square
        )
        total = total + dot_nn(active, wout_ref[cols, :])
    centred = total - mean_rows(total)
    r2 = lax.rsqrt(mean_rows(centred * centred) + EPS)
    n2 = centred * r2
    out_ref[...] = (n2 * g2 + s2).astype(BF16)
    e = cot_ref[...].astype(F32)
    m = e * g2
    second = (m - mean_rows(m) - n2 * mean_rows(m * n2)) * r2
    feed = second.astype(BF16)
    feed_ref[...] = feed
    vecg[6:7] += jnp.sum(e * n2, axis=0, keepdims=True)
    vecg[7:8] += jnp.sum(e, axis=0, keepdims=True)
    vecg[5:6] += jnp.sum(feed.astype(F32), axis=0, keepdims=True)
    e = second
    for c in range(chunks):
        cols = slice(c * CHUNK, (c + 1) * CHUNK)
        inner_grad = (dot_nt(feed, wout_ref[cols, :]) * slope[:, cols]).astype(BF16)
        inner_grad_ref[:, cols] = inner_grad
        ibg[0:1, cols] += jnp.sum(inner_grad.astype(F32), axis=0, keepdims=True)
        e = e + dot_nt(inner_grad, win_ref[:, cols])
    m = e * g1
    first = (m - mean_rows(m) - n1 * mean_rows(m * n1)) * r1
    first_ref[...] = first
    branch = first.astype(BF16)
    branch_ref[...] = branch
    vecg[3:4] += jnp.sum(e * n1, axis=0, keepdims=True)
    vecg[4:5] += jnp.sum(e, axis=0, keepdims=True)
    vecg[2:3] += jnp.sum(branch.astype(F32), axis=0, keepdims=True)
    mixed_ref[...] = dot_nt(branch, wo_ref[...]).astype(BF16)

    @pl.when(step == pl.num_programs(0) - 1)
    def _():
        vecg_ref[...] = jnp.transpose(vecg[...]).astype(BF16)
        ibg_ref[...] = jnp.transpose(ibg[...]).astype(BF16)


def row_stage(x, attended, cotangent, wo, win, wout, vec, ib):
    rows, width = x.shape
    hidden_width = win.shape[1]
    block = min(ROWS, rows)
    whole = lambda a: pl.BlockSpec(a.shape, lambda i: (0, 0), pipeline_mode=pl.Buffered(1))
    narrow = pl.BlockSpec((block, width), lambda i: (i, 0))
    wide = pl.BlockSpec((block, hidden_width), lambda i: (i, 0))
    low = jax.ShapeDtypeStruct((rows, width), BF16)
    low_wide = jax.ShapeDtypeStruct((rows, hidden_width), BF16)
    return pl.pallas_call(
        rows_kernel,
        grid=(rows // block,),
        in_specs=[narrow] * 3 + [whole(a) for a in (wo, win, wout, vec, ib)],
        out_specs=[
            narrow,
            narrow,
            wide,
            wide,
            narrow,
            narrow,
            narrow,
            narrow,
            pl.BlockSpec(vec.shape, lambda i: (0, 0)),
            pl.BlockSpec(ib.shape, lambda i: (0, 0)),
        ],
        out_shape=[
            low,
            low,
            low_wide,
            low_wide,
            low,
            low,
            low,
            jax.ShapeDtypeStruct((rows, width), F32),
            jax.ShapeDtypeStruct(vec.shape, BF16),
            jax.ShapeDtypeStruct(ib.shape, BF16),
        ],
        scratch_shapes=[
            pltpu.VMEM((8, width), F32),
            pltpu.VMEM((8, hidden_width), F32),
            pltpu.VMEM((block, hidden_width), F32),
            pltpu.VMEM((LANES, width), F32),
            pltpu.VMEM((LANES, hidden_width), F32),
        ],
        compiler_params=pltpu.CompilerParams(vmem_limit_bytes=VMEM_LIMIT),
        name="row_stage",
    )(x, attended, cotangent, wo, win, wout, vec, ib)


def product_kernel(left_ref, right_ref, out_ref):
    out_ref[...] = dot_tn(left_ref[...], right_ref[...]).astype(BF16)


def product(left, right, block_m, block_n):
    depth, rows = left.shape
    cols = right.shape[1]
    return pl.pallas_call(
        product_kernel,
        grid=(rows // block_m, cols // block_n),
        in_specs=[
            pl.BlockSpec((depth, block_m), lambda i, j: (0, i)),
            pl.BlockSpec((depth, block_n), lambda i, j: (0, j)),
        ],
        out_specs=pl.BlockSpec((block_m, block_n), lambda i, j: (i, j)),
        out_shape=jax.ShapeDtypeStruct((rows, cols), BF16),
        compiler_params=pltpu.CompilerParams(vmem_limit_bytes=VMEM_LIMIT),
        name="weight_gradient",
    )(left, right)


def input_kernel(first_ref, dq_ref, dk_ref, dv_ref, wq_ref, wk_ref, wv_ref, out_ref, vecg_ref, acc):
    step = pl.program_id(0)

    @pl.when(step == 0)
    def _():
        acc[...] = jnp.zeros_like(acc)

    out_ref[...] = (
        first_ref[...]
        + dot_nt(dq_ref[...], wq_ref[...])
        + dot_nt(dk_ref[...], wk_ref[...])
        + dot_nt(dv_ref[...], wv_ref[...])
    ).astype(BF16)
    acc[0:1] += jnp.sum(dq_ref[...].astype(F32), axis=0, keepdims=True)
    acc[1:2] += jnp.sum(dv_ref[...].astype(F32), axis=0, keepdims=True)

    @pl.when(step == pl.num_programs(0) - 1)
    def _():
        vecg_ref[...] = jnp.transpose(acc[...]).astype(BF16)


def input_stage(first, dq, dk, dv, wq, wk, wv):
    rows, width = first.shape
    block = min(ROWS, rows)
    narrow = pl.BlockSpec((block, width), lambda i: (i, 0))
    whole = pl.BlockSpec((width, width), lambda i: (0, 0))
    return pl.pallas_call(
        input_kernel,
        grid=(rows // block,),
        in_specs=[narrow] * 4 + [whole] * 3,
        out_specs=[narrow, pl.BlockSpec((width, LANES), lambda i: (0, 0))],
        out_shape=[
            jax.ShapeDtypeStruct((rows, width), BF16),
            jax.ShapeDtypeStruct((width, LANES), BF16),
        ],
        scratch_shapes=[pltpu.VMEM((LANES, width), F32)],
        compiler_params=pltpu.CompilerParams(vmem_limit_bytes=VMEM_LIMIT),
        name="input_stage",
    )(first, dq, dk, dv, wq, wk, wv)


def body(
    inputs,
    cotangent,
    query_weight,
    query_bias,
    key_weight,
    value_weight,
    value_bias,
    output_weight,
    output_bias,
    first_gain,
    first_shift,
    inner_weight,
    inner_bias,
    outer_weight,
    outer_bias,
    second_gain,
    second_shift,
):
    micro, _, length, width = inputs.shape
    parts = lax.axis_size("seq")
    boxed = parts == 2 and lax.axis_size("grp") == 16 and query_weight.shape[0] % 8 == 0
    own = inputs[:, 0]
    tokens = own.reshape(-1, width)
    vectors = jnp.stack(
        (
            query_bias,
            value_bias,
            output_bias,
            first_gain,
            first_shift,
            outer_bias,
            second_gain,
            second_shift,
        ),
        axis=1,
    )
    vectors = jnp.pad(vectors, ((0, 0), (0, LANES - vectors.shape[1])))
    inner_column = jnp.pad(inner_bias[:, None], ((0, 0), (0, LANES - 1)))
    shards = (
        query_weight,
        key_weight,
        value_weight,
        vectors,
        output_weight,
        inner_weight,
        inner_column,
        outer_weight,
    )
    if boxed:
        fulls, all_rows = gather_box(shards, own)
    else:
        fulls = [lax.all_gather(a, ("seq", "grp"), axis=0, tiled=True) for a in shards]
        all_rows = lax.all_gather(own, "seq", axis=0)
    wq, wk, wv, vec, wo, win, ib, wout = fulls

    queries, kv = project(own, all_rows, wq, wk, wv, vec)
    attended, lse = attend(queries, kv)
    flat = attended.reshape(-1, width)
    (
        layer_out,
        hidden_low,
        active,
        inner_grad,
        feed_grad,
        branch_grad,
        mixed_grad,
        first_grad,
        vec_grad,
        ib_grad,
    ) = row_stage(tokens, flat, cotangent[:, 0].reshape(-1, width), wo, win, wout, vec, ib)
    wout_grad = product(active, feed_grad, 768, 768)
    win_grad = product(hidden_low, inner_grad, 768, 768)
    wo_grad = product(flat, branch_grad, 768, 768)
    dq, dk, dv = attend_back(queries, kv, attended, mixed_grad.reshape(micro, length, width), lse)
    if boxed:
        s = lax.axis_index("seq")
        flip = [(0, 1), (1, 0)]

        def joined(terms):
            mine = lax.dynamic_index_in_dim(terms, s, 0, keepdims=False)
            other = lax.ppermute(
                lax.dynamic_index_in_dim(terms, 1 - s, 0, keepdims=False), "seq", flip
            )
            return (mine.astype(F32) + other.astype(F32)).astype(BF16)

        dk, dv = joined(dk), joined(dv)
    else:
        dk = lax.psum_scatter(dk, "seq", scatter_dimension=0)
        dv = lax.psum_scatter(dv, "seq", scatter_dimension=0)
    dq, dk, dv = (a.reshape(-1, width) for a in (dq, dk, dv))
    wq_grad = product(tokens, dq, 768, 768)
    wk_grad = product(tokens, dk, 768, 768)
    wv_grad = product(tokens, dv, 768, 768)
    input_grad, vec2_grad = input_stage(first_grad, dq, dk, dv, wq, wk, wv)

    terms = (wout_grad, ib_grad, win_grad, wo_grad, vec_grad, wq_grad, wk_grad, wv_grad, vec2_grad)
    if boxed:
        summed = scatter_box(terms)
    else:
        summed = [
            lax.psum_scatter(a.astype(F32), ("seq", "grp"), scatter_dimension=0, tiled=True)
            for a in terms
        ]
        summed = lax.optimization_barrier(summed)
    wout_s, ib_s, win_s, wo_s, vec_s, wq_s, wk_s, wv_s, vec2_s = summed
    return (
        layer_out.reshape(inputs.shape),
        input_grad.reshape(inputs.shape),
        wq_s,
        vec2_s[:, 0],
        wk_s,
        wv_s,
        vec2_s[:, 1],
        wo_s,
        vec_s[:, 2],
        vec_s[:, 3],
        vec_s[:, 4],
        win_s,
        ib_s[:, 0],
        wout_s,
        vec_s[:, 5],
        vec_s[:, 6],
        vec_s[:, 7],
    )


def solution(mesh):
    rows = P(("seq", "grp"), None)
    line = P(("seq", "grp"))
    tokens = P(None, "grp", "seq", None)
    return jax.shard_map(
        body,
        mesh=mesh,
        in_specs=(
            tokens,
            tokens,
            rows,
            line,
            rows,
            rows,
            line,
            rows,
            line,
            line,
            line,
            rows,
            line,
            rows,
            line,
            line,
            line,
        ),
        out_specs=(
            tokens,
            tokens,
            rows,
            line,
            rows,
            rows,
            line,
            rows,
            line,
            line,
            line,
            rows,
            line,
            rows,
            line,
            line,
            line,
        ),
        check_vma=False,
    )
```

time: 1380 us -> 414 us (0.30)
  waiting for transfers between devices: 803 us -> 0.01 us
  Pallas kernels: 0 us -> 387 us
  matrix products: 309 us -> 0 us
  local copies, waits for them, and re-layouts: 113 us -> 18.7 us
  blocking collectives: 80.1 us -> 0 us
  other arithmetic: 50.5 us -> 6.79 us
  between operations: 16.3 us -> 0.71 us
    pallas_call x0 -> x13, Pallas kernels: none -> 387 us  [the longest x1 117 us: gather_box(): pl.pallas_call(functools.partial(gather_kernel, count), out_shape=[jax.Sh...]
    unnamed x23 -> x0, waiting for transfers between devices: 317 us -> none
    dot_general x72 -> x0, matrix products: 309 us -> none  [the longest x12 54.3 us: block_scores(): jnp.einsum('qhd,khd->hqk', queries, key_block, preferred_element_type=jnp...]
    reduce_scatter x7 -> x0, waiting for transfers between devices: 285 us -> none  [the longest x3 285 us: body(): lax.psum_scatter(gradients, ('seq', 'grp'), scatter_dimension=0, tiled=True)]
    all_gather x10 -> x0, waiting for transfers between devices: 201 us -> none  [the longest x1 58.2 us: body(): lax.all_gather(shards[2], ('seq', 'grp'), axis=0, tiled=True)]
    unnamed x2 -> x0, blocking collectives: 80.1 us -> none
    unnamed x243 -> x10, local copies, waits for them, and re-layouts: 61 us -> 8.5 us
    reduce_sum x20 -> x0, other arithmetic: 39.9 us -> none  [the longest x4 28 us: running(): jnp.sum(jnp.exp(scores - new_top[..., None]), axis=-1)]
  transfers between devices with their start and end apart: 20 -> 2, of which waited for: 12 -> 0; matrix products, arithmetic and copies ran while one was open for 23% -> 1% of each run, Pallas kernels for 0% -> 8%
where the time goes in v1:
time: 414 us; the launch traced here: 413 us
  Pallas kernels  387 us (93%)
  local copies, waits for them, and re-layouts  18.7 us (5%)
  other arithmetic  6.79 us (2%)
    pallas_call x1, Pallas kernels, gather_box(): pl.pallas_call(functools.partial(gather_kernel, count), out_shape=[jax.Sh...  117 us
    pallas_call x1, Pallas kernels, scatter_box(): pl.pallas_call(functools.partial(scatter_kernel, count), out_shape=[jax.S...  110 us
    pallas_call x1, Pallas kernels, row_stage(): pl.pallas_call(rows_kernel, grid=(rows // block,), in_specs=[narrow] * 3...  40.9 us
    pallas_call x1, Pallas kernels, attend_back(): pl.pallas_call(attend_back_kernel, grid=(micro, pairs), in_specs=[row, co...  37.1 us
    pallas_call x6, Pallas kernels, product(): pl.pallas_call(product_kernel, grid=(rows // block_m, cols // block_n), i...  35.9 us
    pallas_call x1, Pallas kernels, attend(): pl.pallas_call(attend_kernel, grid=(micro, pairs), in_specs=[pl.BlockSpec...  25.8 us
    pallas_call x1, Pallas kernels, project(): pl.pallas_call(project_kernel, grid=(parts * micro,), in_specs=[pl.BlockS...  11.4 us
    pallas_call x1, Pallas kernels, input_stage(): pl.pallas_call(input_kernel, grid=(rows // block,), in_specs=[narrow] * 4...  9.01 us
  transfers between devices with their start and end apart: 2, of which 0 were waited for; matrix products, arithmetic and copies ran while one was open for 1% of the time, Pallas kernels for 8%

profile of v1, /device:TPU:0, one launch (start us, length us, event | category | flops | bytes accessed | tf_op | source)
XLA Modules:
  0.0 413.2 jit_solution(14881708391355658863)
XLA Ops:
  3.5 116.6 %gather_weights.1 = (bf16[2,4,2,2,24,768]{5,4,3,2,1,0:T(8,128)(2,1)}, bf16[2,4,2,2,24,768]{5,4,3,2,1,0:T(8,128)(2,1)}, bf16[2,4,2,2,24,768]{5,4,3,2,1,0:T(8,128)...) custom-call(bf16[24,768]{1,0:T(8,128)(2,1)} %refs_0_.1, ...), custom_call_target="tpu_custom_call" | custom-call | tf_op jit(solution)/shard_map/gather_weights/pallas_call | solution.py:153
  120.1 11.4 %project.1 = (bf16[2,512,768]{2,1,0:T(8,128)(2,1)}, bf16[2,2,512,1536]{3,2,1,0:T(8,128)(2,1)}) custom-call(bf16[2,512,768]{2,1,0:T(8,128)(2,1)} %bitcast.51, bf16[2,2,512,768]{3,2,1,0:T(8,128)(2,1)} %get-tuple-element.54.all_ref, bf16[768,768]{1,0:T(8,128)(2,1)} %bitcast.68, bf16[768,768]{1,0:T(8,128)(2,1)} %bitcast.70, bf16[768,768]{1,0:T(8,128)(2,1)} %bitcast.72, ...), custom_call_target="tpu_custom_call" | custom-call | tf_op jit(solution)/shard_map/project/pallas_call | solution.py:348
  131.5 25.8 %attend.1 = (bf16[2,512,768]{2,1,0:T(8,128)(2,1)}, f32[2,6,2,512]{3,2,1,0:T(2,128)}) custom-call(bf16[2,512,768]{2,1,0:T(8,128)(2,1)} %get-tuple-element.59.q_ref, bf16[2,2,512,1536]{3,2,1,0:T(8,128)(2,1)} %get-tuple-element.60.k_ref.v_ref, bf16[2,2,512,1536]{3,2,1,0:T(8,128)(2,1)} %get-tuple-element.60.k_ref.v_ref), custom_call_target="tpu_custom_call" | custom-call | tf_op jit(solution)/shard_map/attend/pallas_call | solution.py:402
  157.2 40.9 %row_stage.1 = (bf16[1024,768]{1,0:T(8,128)(2,1)}, bf16[1024,768]{1,0:T(8,128)(2,1)}, bf16[1024,3072]{1,0:T(8,128)(2,1)}, bf16[1024,3072]{1,0:T(8,128)(2,1)}, bf...) custom-call(bf16[1024,768]{1,0:T(8,128)(2,1)} %bitcast.52, ...), custom_call_target="tpu_custom_call" | custom-call | tf_op jit(solution)/shard_map/row_stage/pallas_call | solution.py:585
  198.1 37.1 %attend_back.1 = (bf16[2,512,768]{2,1,0:T(8,128)(2,1)}, bf16[2,2,512,768]{3,2,1,0:T(8,128)(2,1)}, bf16[2,2,512,768]{3,2,1,0:T(8,128)(2,1)}) custom-call(bf16[2,512,768]{2,1,0:T(8,128)(2,1)} %get-tuple-element.59.q_ref, bf16[2,2,512,1536]{3,2,1,0:T(8,128)(2,1)} %get-tuple-element.60.k_ref.v_ref, bf16[2,2,512,1536]{3,2,1,0:T(8,128)(2,1)} %get-tuple-element.60.k_ref.v_ref, ...), custom_call_target="tpu_custom_call" | custom-call | tf_op jit(solution)/shard_map/attend_back/pallas_call | solution.py:459
  235.2 2.8 dynamic-slice_bitcast_fusion
  238.5 1.2 dynamic-slice_bitcast_fusion.1
  239.7 4.4 %weight_gradient.8 = bf16[768,768]{1,0:T(8,128)(2,1)} custom-call(bf16[1024,768]{1,0:T(8,128)(2,1)} %bitcast.63, bf16[1024,768]{1,0:T(8,128)(2,1)} %get-tuple-element.79.right_ref), custom_call_target="tpu_custom_call" | custom-call | tf_op jit(solution)/shard_map/weight_gradient/pallas_call | solution.py:632
  244.1 4.4 %weight_gradient.9 = bf16[768,768]{1,0:T(8,128)(2,1)} custom-call(bf16[1024,768]{1,0:T(8,128)(2,1)} %bitcast.53, bf16[1024,768]{1,0:T(8,128)(2,1)} %bitcast.64), custom_call_target="tpu_custom_call" | custom-call | tf_op jit(solution)/shard_map/weight_gradient/pallas_call | solution.py:632
  248.5 9.2 %weight_gradient.7 = bf16[768,3072]{1,0:T(8,128)(2,1)} custom-call(bf16[1024,768]{1,0:T(8,128)(2,1)} %get-tuple-element.77.left_ref, bf16[1024,3072]{1,0:T(8,128)(2,1)} %get-tuple-element.78.right_ref), custom_call_target="tpu_custom_call" | custom-call | tf_op jit(solution)/shard_map/weight_gradient/pallas_call | solution.py:632
  257.8 9.2 %weight_gradient.6 = bf16[3072,768]{1,0:T(8,128)(2,1)} custom-call(bf16[1024,3072]{1,0:T(8,128)(2,1)} %get-tuple-element.74.left_ref, bf16[1024,768]{1,0:T(8,128)(2,1)} %get-tuple-element.75.right_ref), custom_call_target="tpu_custom_call" | custom-call | tf_op jit(solution)/shard_map/weight_gradient/pallas_call | solution.py:632
  267.0 3.4 fusion
  270.4 4.4 %weight_gradient.11 = bf16[768,768]{1,0:T(8,128)(2,1)} custom-call(bf16[1024,768]{1,0:T(8,128)(2,1)} %bitcast.54, bf16[1024,768]{1,0:T(8,128)(2,1)} %bitcast.58), custom_call_target="tpu_custom_call" | custom-call | tf_op jit(solution)/shard_map/weight_gradient/pallas_call | solution.py:632
  274.7 3.4 fusion.1
  278.1 4.4 %weight_gradient.10 = bf16[768,768]{1,0:T(8,128)(2,1)} custom-call(bf16[1024,768]{1,0:T(8,128)(2,1)} %bitcast.55, bf16[1024,768]{1,0:T(8,128)(2,1)} %bitcast.60), custom_call_target="tpu_custom_call" | custom-call | tf_op jit(solution)/shard_map/weight_gradient/pallas_call | solution.py:632
  282.5 9.0 %input_stage.1 = (bf16[1024,768]{1,0:T(8,128)(2,1)}, bf16[768,128]{1,0:T(8,128)(2,1)}) custom-call(f32[1024,768]{1,0:T(8,128)} %get-tuple-element.67.first_ref, bf16[1024,768]{1,0:T(8,128)(2,1)} %bitcast.65, bf16[1024,768]{1,0:T(8,128)(2,1)} %bitcast.61, bf16[1024,768]{1,0:T(8,128)(2,1)} %bitcast.59, bf16[768,768]{1,0:T(8,128)(2,1)} %bitcast.69, ...), custom_call_target="tpu_custom_call" | custom-call | tf_op jit(solution)/shard_map/input_stage/pallas_call | solution.py:672
  291.5 110.0 %scatter_gradients.1 = (f32[96,768]{1,0:T(8,128)}, f32[96,128]{1,0:T(8,128)}, f32[24,3072]{1,0:T(8,128)}, f32[24,768]{1,0:T(8,128)}, f32[24,128]{1,0:T(8,128)}, ...) custom-call(bf16[2,4,2,2,96,768]{5,4,3,2,1,0:T(8,128)(2,1)} %bitcast.57, ...), custom_call_target="tpu_custom_call" | custom-call | tf_op jit(solution)/shard_map/scatter_gradients/pallas_call | solution.py:312
  401.5 1.5 slice_reduce_fusion
  403.0 1.8 slice_reduce_fusion.1
  404.8 1.5 copy.66
  406.3 1.5 copy.67
  407.8 1.5 copy.68
  409.3 1.5 copy.69
  410.8 1.7 copy.70
  (14 shorter events, 4.1 us)
Async XLA Ops:
  235.2 3.3 copy-start
  238.0 29.0 %collective-permute-start.1 = (bf16[2,512,768]{2,1,0:T(8,128)(2,1)}, bf16[2,512,768]{2,1,0:T(8,128)(2,1)}, u32[]{:S(2)}, u32[]{:S(2)}) collective-permute-start(bf16[2,512,768]{2,1,0:T(8,128)(2,1)} %dynamic-slice_bitcast_fusion), channel_id=1, source_target_pairs={{0,16},{16,0},{1,17},{17,1},{2,18},{18,2},{3,19},{19,3},{4,20},{20... | collective-permute-start | bytes 4718600 | tf_op jit(solution)/shard_map/ppermute | solution.py:768
  239.7 35.0 %collective-permute-start = (bf16[2,512,768]{2,1,0:T(8,128)(2,1)}, bf16[2,512,768]{2,1,0:T(8,128)(2,1)}, u32[]{:S(2)}, u32[]{:S(2)}) collective-permute-start(bf16[2,512,768]{2,1,0:T(8,128)(2,1)} %dynamic-slice_bitcast_fusion.1), channel_id=1, source_target_pairs={{0,16},{16,0},{1,17},{17,1},{2,18},{18,2},{3,19},{19,3},{4,20},{20... | collective-permute-start | bytes 4718600 | tf_op jit(solution)/shard_map/ppermute | solution.py:768
  401.5 11.0 %copy-start.1 = (f32[96,768]{1,0:T(8,128)S(1)}, f32[96,768]{1,0:T(8,128)}, u32[]{:S(2)}) copy-start(f32[96,768]{1,0:T(8,128)} %get-tuple-element.182) | copy-start | bytes 884740
